TPU v7x, 32 devices: a whole 2x2x4 slice. The times are simulated.
32 devices in a mesh: row: 8 (over z, x), col: 4 (over y, core).
Axes of the slice: x: 2, y: 2, z: 4, core: 2. Of those that a mesh axis runs over, the one named last changes fastest.
Arguments:
- features: bfloat16 [14336, 2048], P('row', 'col'), may hold values from -6 to 6
- neighbours: int32 [14336, 32], P('row'), may hold values from -1 to 127, as said below
- node_valid: int32 [14336], P('row'), may hold values from 0 to 1, as said below
- weight_one: bfloat16 [2048, 2048], P(None, 'col'), may hold values from -0.125 to 0.125
- gamma_one: float32 [2048], P('col'), may hold values from 0.25 to 1.75
- beta_one: float32 [2048], P('col'), may hold values from -0.5 to 0.5
- weight_two: bfloat16 [2048, 2048], P(None, 'col'), may hold values from -0.125 to 0.125
- gamma_two: float32 [2048], P('col'), may hold values from 0.25 to 1.75
- beta_two: float32 [2048], P('col'), may hold values from -0.5 to 0.5
- cotangent: bfloat16 [14336, 2048], P('row', 'col'), may hold values from -6 to 6
Outputs:
- output: float32 [14336, 2048], P('row', 'col')
- grad_features: float32 [14336, 2048], P('row', 'col')
- grad_weight_one: float32 [2048, 2048], P(None, 'col')
- grad_gamma_one: float32 [2048], P('col')
- grad_beta_one: float32 [2048], P('col')
- grad_weight_two: float32 [2048, 2048], P(None, 'col')
- grad_gamma_two: float32 [2048], P('col')
- grad_beta_two: float32 [2048], P('col')
Inputs may be any that keep to these rules, and one draw needn't show every extreme that they name: `neighbours`: entries >= 0 name valid nodes of the same slot; every valid node has 1 to 32 such entries, first in its list, the rest are -1; a padding row has only -1; some slot is full. `node_valid`: in each slot the valid nodes come first and number at least 40.
All inputs are finite; a program needn't handle non-finite values.
Results may differ from a plain program's by a relative error of at most 0.012.
Values may be sent and summed in bfloat16 or wider, within the bound.
No kernel may reach another device: no remote copies, remote signals or barrier semaphores. Data moves between devices by JAX's collectives and lax.ppermute only.
A program may use at most 128 MiB of HBM per device.

v0:
```python
import jax
import jax.numpy as jnp
from jax import lax
from jax.sharding import PartitionSpec as P

SLOT = 128
NBR = 32
EPSILON = 1e-05


def build_tiles(neighbours):
    entries_all = neighbours.reshape(-1, SLOT, NBR)

    def build(entries):
        columns = jnp.arange(SLOT, dtype=jnp.int32)
        hits = jnp.sum((entries[:, :, None] == columns[None, None, :]).astype(jnp.float32), axis=1)
        degree = jnp.sum((entries >= 0).astype(jnp.float32), axis=1)
        joined = hits + jnp.eye(SLOT, dtype=jnp.float32)
        return joined / (degree[:, None] + 1.0)

    tiles = lax.map(build, entries_all)
    return (tiles, jnp.diagonal(tiles, axis1=1, axis2=2))


def spread(values, tiles, self_weight):
    shaped = values.reshape(tiles.shape[0], SLOT, values.shape[1])
    summed = jnp.einsum("sij,sjd->sid", tiles, shaped, precision=lax.Precision.HIGHEST)
    return (summed + self_weight[:, :, None] * shaped).reshape(values.shape)


def spread_back(grads, tiles, self_weight):
    shaped = grads.reshape(tiles.shape[0], SLOT, grads.shape[1])
    summed = jnp.einsum("sji,sjd->sid", tiles, shaped, precision=lax.Precision.HIGHEST)
    return (summed + self_weight[:, :, None] * shaped).reshape(grads.shape)


def moments(linear, valid):
    total_valid, summed = lax.psum((jnp.sum(valid), jnp.sum(valid * linear, axis=0)), "row")
    mean = summed / total_valid
    centred = linear - mean
    variance = lax.psum(jnp.sum(valid * centred * centred, axis=0), "row") / total_valid
    return (total_valid, mean, variance)


def forward_layer(values, weight, gamma, beta, tiles, self_weight, valid):
    mixed = spread(values, tiles, self_weight).astype(jnp.bfloat16)
    gathered = lax.all_gather(mixed, "col", axis=1, tiled=True)
    linear = jnp.dot(gathered, weight, preferred_element_type=jnp.float32)
    total_valid, mean, variance = moments(linear, valid)
    inv_std = lax.rsqrt(variance + EPSILON)
    normed = (linear - mean) * inv_std
    before = gamma * normed + beta
    result = valid * jax.nn.silu(before)
    return (result, (gathered, normed, inv_std, before, total_valid))


def backward_layer(grad_result, weight, gamma, kept, tiles, self_weight, valid):
    gathered, normed, inv_std, before, total_valid = kept
    sigmoid_value = jax.nn.sigmoid(before)
    slope = sigmoid_value * (1.0 + before * (1.0 - sigmoid_value))
    grad_before = grad_result * valid * slope
    grad_beta, grad_gamma = lax.psum(
        (jnp.sum(grad_before, axis=0), jnp.sum(grad_before * normed, axis=0)), "row"
    )
    grad_normed = gamma * grad_before
    grad_linear = inv_std * (
        grad_normed - valid * (gamma * grad_beta + normed * gamma * grad_gamma) / total_valid
    )
    grad_low = grad_linear.astype(jnp.bfloat16)
    weight_terms = lax.dot_general(
        gathered, grad_low, (((0,), (0,)), ((), ())), preferred_element_type=jnp.float32
    )
    grad_weight = lax.psum(weight_terms, "row")
    partial_terms = lax.dot_general(
        grad_low, weight, (((1,), (1,)), ((), ())), preferred_element_type=jnp.float32
    )
    grad_mixed = lax.psum_scatter(partial_terms, "col", scatter_dimension=1, tiled=True)
    grad_values = spread_back(grad_mixed, tiles, self_weight)
    return (grad_values, grad_weight, grad_gamma, grad_beta)


def local(
    features,
    neighbours,
    node_valid,
    weight_one,
    gamma_one,
    beta_one,
    weight_two,
    gamma_two,
    beta_two,
    cotangent,
):
    tiles, self_weight = build_tiles(neighbours)
    valid = node_valid.astype(jnp.float32)[:, None]
    hidden, kept_one = forward_layer(
        features.astype(jnp.float32), weight_one, gamma_one, beta_one, tiles, self_weight, valid
    )
    output, kept_two = forward_layer(
        hidden, weight_two, gamma_two, beta_two, tiles, self_weight, valid
    )
    grad_hidden, grad_weight_two, grad_gamma_two, grad_beta_two = backward_layer(
        cotangent.astype(jnp.float32), weight_two, gamma_two, kept_two, tiles, self_weight, valid
    )
    grad_features, grad_weight_one, grad_gamma_one, grad_beta_one = backward_layer(
        grad_hidden, weight_one, gamma_one, kept_one, tiles, self_weight, valid
    )
    return (
        output,
        grad_features,
        grad_weight_one,
        grad_gamma_one,
        grad_beta_one,
        grad_weight_two,
        grad_gamma_two,
        grad_beta_two,
    )


def solution(mesh):
    placed = (
        P("row", "col"),
        P("row", None),
        P("row"),
        P(None, "col"),
        P("col"),
        P("col"),
        P(None, "col"),
        P("col"),
        P("col"),
        P("row", "col"),
    )
    return jax.shard_map(
        local,
        mesh=mesh,
        in_specs=placed,
        out_specs=(
            P("row", "col"),
            P("row", "col"),
            P(None, "col"),
            P("col"),
            P("col"),
            P(None, "col"),
            P("col"),
            P("col"),
        ),
        check_vma=False,
    )
```

profile of v0, /device:TPU:0, one launch (start us, length us, event | category | flops | bytes accessed | tf_op | source)
XLA Modules:
  0.0 855.5 jit_solution(2408295498759646820)
XLA Ops:
  7.3 2.3 copy.23
  9.6 27.6 %while.10 = (s32[]{:T(128)}, f32[14,128,128]{2,1,0:T(8,128)S(1)}, s32[14,128,32]{2,1,0:T(8,128)}, s32[]{:T(128)}) while((s32[]{:T(128)}, f32[14,128,128]{2,1,0:T(8,128)S(1)}, s32[14,128,32]{2,1,0:T(8,128)}, s32[]{:T(128)}) %tuple.47), condition=%wide.region_3.4_spmd, body=%wide.region_0.3_spmd.sunk | while | flops 1634306 | bytes 247877 | solution.py:21
  9.6 0.9 convert_reduce_fusion.5
  10.5 0.9 convert_reduce_fusion.6
  11.5 0.9 convert_reduce_fusion.5
  12.5 0.9 convert_reduce_fusion.6
  13.5 0.9 convert_reduce_fusion.5
  14.4 0.9 convert_reduce_fusion.6
  15.5 0.9 convert_reduce_fusion.5
  16.4 0.9 convert_reduce_fusion.6
  17.4 0.9 convert_reduce_fusion.5
  18.4 0.9 convert_reduce_fusion.6
  19.4 0.9 convert_reduce_fusion.5
  20.4 0.9 convert_reduce_fusion.6
  21.4 0.9 convert_reduce_fusion.5
  22.3 0.9 convert_reduce_fusion.6
  23.4 0.9 convert_reduce_fusion.5
  24.3 0.9 convert_reduce_fusion.6
  25.3 0.9 convert_reduce_fusion.5
  26.3 0.9 convert_reduce_fusion.6
  27.3 0.9 convert_reduce_fusion.5
  28.3 0.9 convert_reduce_fusion.6
  29.3 0.9 convert_reduce_fusion.5
  30.2 0.9 convert_reduce_fusion.6
  31.3 0.9 convert_reduce_fusion.5
  32.2 0.9 convert_reduce_fusion.6
  33.2 0.9 convert_reduce_fusion.5
  34.2 0.9 convert_reduce_fusion.6
  35.2 0.9 convert_reduce_fusion.5
  36.2 0.9 convert_reduce_fusion.6
  37.2 4.7 copy.24
  41.8 1.8 gather_fusion
  43.7 5.1 add_convert_fusion.1
  49.5 54.5 %all-gather.3.cloned.1.call-done = bf16[1792,2048]{1,0:T(8,128)(2,1)} async-done(((bf16[1792,512]{1,0:T(8,128)(2,1)}), bf16[1792,2048]{1,0:T(8,128)(2,1)}) %all-gather.3.cloned.1.call-update) | async-done | bytes 7340048 | tf_op jit(solution)/shard_map/all_gather | solution.py:47
  104.0 9.5 %multiply_reduce_fusion.3 = (f32[512]{0:T(512)S(1)}, f32[1792,512]{1,0:T(8,128)}) fusion(f32[1792]{0:T(1024)S(1)} %convert_element_type.41, bf16[1792,2048]{1,0:T(8,128)(2,1)} %all-gather.3.cloned.1.call-done, bf16[2048,512]{1,0:T(8,128)(2,1)} %param.15), kind=kOutput, calls=%fused_computation.29 | convolution fusion | flops 3759930880 | bytes 13116416 | tf_op jit(solution)/shard_map/dot_general | solution.py:48
  113.5 22.0 %all-reduce.2 = (f32[512]{0:T(512)S(1)}, f32[]{:T(128)}) all-reduce(f32[512]{0:T(512)S(1)} %get-tuple-element.49, f32[]{:T(128)} %convert_reduce_fusion.2), channel_id=1, replica_groups=mesh['row'=8,'col'=4] {'row'}, use_global_device_ids=true, to_apply=%region_5.6 | all-reduce | flops 513 | bytes 4104 | tf_op jit(solution)/shard_map/psum | solution.py:38
  136.0 2.6 fusion.2
  138.6 17.1 %psum.82 = f32[512]{0:T(512)S(1)} all-reduce(f32[512]{0:T(512)S(1)} %fusion.2), channel_id=1, replica_groups=mesh['row'=8,'col'=4] {'row'}, use_global_device_ids=true, to_apply=%region_9.10 | all-reduce | flops 512 | bytes 4096 | tf_op jit(solution)/shard_map/psum | solution.py:41
  156.3 3.0 multiply_multiply_fusion.4
  159.4 4.5 add_convert_fusion
  164.1 50.0 %all-gather.5.cloned.1.call-done = bf16[1792,2048]{1,0:T(8,128)(2,1)} async-done(((bf16[1792,512]{1,0:T(8,128)(2,1)}), bf16[1792,2048]{1,0:T(8,128)(2,1)}) %all-gather.5.cloned.1.call-update) | async-done | bytes 7340048 | tf_op jit(solution)/shard_map/all_gather | solution.py:47
  214.1 8.9 %multiply_reduce_fusion.2 = (f32[512]{0:T(512)S(1)}, f32[1792,512]{1,0:T(8,128)}) fusion(f32[1792]{0:T(1024)S(1)} %convert_element_type.41, bf16[1792,2048]{1,0:T(8,128)(2,1)} %all-gather.5.cloned.1.call-done, bf16[2048,512]{1,0:T(8,128)(2,1)S(1)} %copy-done), kind=kOutput, calls=%fused_computation.25 | convolution fusion | flops 3759930880 | bytes 13116416 | tf_op jit(solution)/shard_map/dot_general | solution.py:48
  223.0 21.5 %psum.83 = f32[512]{0:T(512)S(1)} all-reduce(f32[512]{0:T(512)S(1)} %get-tuple-element.51), channel_id=1, replica_groups=mesh['row'=8,'col'=4] {'row'}, use_global_device_ids=true, to_apply=%region_11.12 | all-reduce | flops 512 | bytes 4096 | tf_op jit(solution)/shard_map/psum | solution.py:38
  245.1 2.6 fusion.3
  247.7 17.1 %psum.84 = f32[512]{0:T(512)S(1)} all-reduce(f32[512]{0:T(512)S(1)} %fusion.3), channel_id=1, replica_groups=mesh['row'=8,'col'=4] {'row'}, use_global_device_ids=true, to_apply=%region_13.14 | all-reduce | flops 512 | bytes 4096 | tf_op jit(solution)/shard_map/psum | solution.py:41
  265.4 6.3 fusion.6
  271.7 19.1 %all-reduce.1 = (f32[512]{0:T(512)S(1)}, f32[512]{0:T(512)S(1)}) all-reduce(f32[512]{0:T(512)S(1)} %get-tuple-element.29, f32[512]{0:T(512)S(1)} %get-tuple-element.28), channel_id=1, replica_groups=mesh['row'=8,'col'=4] {'row'}, use_global_device_ids=true, to_apply=%region_17.18 | all-reduce | flops 1024 | bytes 8192 | tf_op jit(solution)/shard_map/psum | solution.py:62
  290.8 4.5 multiply_convert_fusion.1
  295.4 1.2 copy-done.4
  296.6 7.2 fusion.8
  304.1 109.0 %reduce-scatter.3.cloned.1.call-done = f32[1792,512]{1,0:T(8,128)} async-done(((f32[1792,2048]{1,0:T(8,128)}), f32[1792,512]{1,0:T(8,128)}) %reduce-scatter.3.cloned.1.call-update) | async-done | bytes 3670032 | tf_op jit(solution)/shard_map/reduce_scatter | solution.py:77
  413.1 6.8 multiply_add_fusion.1
  419.9 3.7 fusion.5
  423.7 21.3 %all-reduce = (f32[512]{0:T(512)S(1)}, f32[512]{0:T(512)S(1)}) all-reduce(f32[512]{0:T(512)S(1)} %get-tuple-element.27, f32[512]{0:T(512)S(1)} %get-tuple-element.26), channel_id=1, replica_groups=mesh['row'=8,'col'=4] {'row'}, use_global_device_ids=true, to_apply=%region_22.23 | all-reduce | flops 1024 | bytes 8192 | tf_op jit(solution)/shard_map/psum | solution.py:62
  445.0 4.7 multiply_convert_fusion
  449.8 7.3 fusion.9
  457.4 1.2 copy-done.5
  458.5 9.9 %fusion.11 = f32[2048,512]{1,0:T(8,128)} fusion(bf16[1792,2048]{1,0:T(8,128)(2,1)} %all-gather.5.cloned.1.call-done, bf16[1792,512]{1,0:T(8,128)(2,1)S(1)} %copy-done.5), kind=kOutput, calls=%fused_computation.44 | convolution fusion | flops 3758096384 | bytes 13369344 | tf_op jit(solution)/shard_map/dot_general | solution.py:70
  468.4 10.5 %fusion.10 = f32[2048,512]{1,0:T(8,128)} fusion(bf16[1792,2048]{1,0:T(8,128)(2,1)} %all-gather.3.cloned.1.call-done, bf16[1792,512]{1,0:T(8,128)(2,1)S(1)} %copy-done.7), kind=kOutput, calls=%fused_computation.43 | convolution fusion | flops 3758096384 | bytes 13369344 | tf_op jit(solution)/shard_map/dot_general | solution.py:70
  479.0 87.5 %reduce-scatter.5.cloned.1.call-done = f32[1792,512]{1,0:T(8,128)} async-done(((f32[1792,2048]{1,0:T(8,128)}), f32[1792,512]{1,0:T(8,128)}) %reduce-scatter.5.cloned.1.call-update) | async-done | bytes 3670032 | tf_op jit(solution)/shard_map/reduce_scatter | solution.py:77
  566.5 8.5 multiply_add_fusion
  575.0 267.1 %all-reduce.6.cloned.1.call-done = (f32[2048,512]{1,0:T(8,128)}, f32[2048,512]{1,0:T(8,128)}) async-done(((f32[2048,512]{1,0:T(8,128)}, f32[2048,512]{1,0:T(8,128)}), (f32[2048,512]{1,0:T(8,128)}, f32[2048,512]{1,0:T(8,128)})) %all-reduce.6.cloned.1.call-update) | async-done | bytes 8388624 | tf_op jit(solution)/shard_map/psum | solution.py:73
  842.1 4.8 copy.41
  846.9 2.0 copy.42
  (83 shorter events, 5.3 us)
Async XLA Ops:
  7.2 207.0 %copy-start = (bf16[2048,512]{1,0:T(8,128)(2,1)S(1)}, bf16[2048,512]{1,0:T(8,128)(2,1)}, u32[]{:S(2)}) copy-start(bf16[2048,512]{1,0:T(8,128)(2,1)} %param.18) | copy-start | bytes 6291460
  7.2 96.8 %all-gather.3.cloned.1.call-start = ((), (), s32[]{:S(2)}) async-start(), calls=%async_computation.2 | async-start | bytes 9175040 | tf_op jit(solution)/shard_map/all_gather | solution.py:47
  41.8 7.0 copy-start.8
  48.8 165.3 %all-gather.5.cloned.1.call-start = ((), (), s32[]{:S(2)}) async-start(), calls=%async_computation.3 | async-start | bytes 9175040 | tf_op jit(solution)/shard_map/all_gather | solution.py:47
  113.5 42.8 %copy-start.9 = (f32[512]{0:T(512)S(1)}, f32[512]{0:T(512)}, u32[]{:S(2)}) copy-start(f32[512]{0:T(512)} %param.16) | copy-start | bytes 6148
  113.5 42.8 %copy-start.11 = (f32[512]{0:T(512)S(1)}, f32[512]{0:T(512)}, u32[]{:S(2)}) copy-start(f32[512]{0:T(512)} %param.17) | copy-start | bytes 6148
  163.9 249.3 %reduce-scatter.3.cloned.1.call-start = ((), (), s32[]{:S(2)}) async-start(), calls=%async_computation.4 | async-start | bytes 18350080 | tf_op jit(solution)/shard_map/reduce_scatter | solution.py:77
  223.0 42.3 %copy-start.10 = (f32[512]{0:T(512)S(1)}, f32[512]{0:T(512)}, u32[]{:S(2)}) copy-start(f32[512]{0:T(512)} %param.19) | copy-start | bytes 6148
  223.0 42.3 %copy-start.12 = (f32[512]{0:T(512)S(1)}, f32[512]{0:T(512)}, u32[]{:S(2)}) copy-start(f32[512]{0:T(512)} %param.20) | copy-start | bytes 6148
  290.8 4.5 copy-start.13
  290.8 4.6 copy-start.15
  295.3 1.2 copy-start.4
  303.8 262.6 %reduce-scatter.5.cloned.1.call-start = ((), (), s32[]{:S(2)}) async-start(), calls=%async_computation.5 | async-start | bytes 18350080 | tf_op jit(solution)/shard_map/reduce_scatter | solution.py:77
  413.1 6.8 copy-start.2
  445.0 4.7 copy-start.14
  445.0 4.7 copy-start.16
  445.0 4.7 copy-start.17
  449.7 7.3 copy-start.6
  457.0 1.5 copy-start.5
  457.0 385.1 %all-reduce.6.cloned.1.call-start = ((), (), s32[]{:S(2)}) async-start(), calls=%async_computation.6 | async-start | bytes 16777216 | tf_op jit(solution)/shard_map/psum | solution.py:73
  458.5 9.9 %copy-start.7 = (bf16[1792,512]{1,0:T(8,128)(2,1)S(1)}, bf16[1792,512]{1,0:T(8,128)(2,1)}, u32[]{:S(2)}) copy-start(bf16[1792,512]{1,0:T(8,128)(2,1)} %copy-done.6) | copy-start | bytes 5505028
  842.1 4.8 copy-start.3
  842.1 6.8 copy-start.1
Sparse Core Ops, SparseCore 0:
  48.9 55.0 all-gather.2
  164.0 50.1 all-gather.4
  303.9 109.1 reduce-scatter.2
  457.2 109.2 reduce-scatter.4
  571.0 271.0 all-reduce.5
where the time goes:
time: 857 us; the launch traced here: 855 us
  waiting for transfers between devices  568 us (66%)
  blocking collectives  118 us (14%)
  matrix products  78.2 us (9%)
  other arithmetic  57.2 us (7%)
  local copies, waits for them, and re-layouts  18.1 us (2%)
  between operations  14 us (2%)
    psum x1, waiting for transfers between devices, backward_layer(): grad_weight = lax.psum(weight_terms, 'row')  267 us
    reduce_scatter x2, waiting for transfers between devices, backward_layer(): lax.psum_scatter(partial_terms, 'col', scatter_dimension=1, tiled=True)  197 us
    all_gather x2, waiting for transfers between devices, forward_layer(): gathered = lax.all_gather(mixed, 'col', axis=1, tiled=True)  105 us
    psum x2, blocking collectives, moments(): lax.psum((jnp.sum(valid), jnp.sum(valid * linear, axis=0)), 'row')  43.4 us
    psum x2, blocking collectives, backward_layer(): lax.psum((jnp.sum(grad_before, axis=0), jnp.sum(grad_before * normed, axi...  40.5 us
    psum x2, blocking collectives, moments(): lax.psum(jnp.sum(valid * centred * centred, axis=0), 'row') / total_valid  34.3 us
    dot_general x2, matrix products, backward_layer(): lax.dot_general(gathered, grad_low, (((0,), (0,)), ((), ())), preferred_e...  20.4 us
    dot_general x2, matrix products, forward_layer(): linear = jnp.dot(gathered, weight, preferred_element_type=jnp.float32)  18.4 us
  transfers between devices with their start and end apart: 5, of which 5 were waited for; matrix products, arithmetic and copies ran while one was open for 3% of the time, Pallas kernels for 0%

commit v1 on v0

--- a/solution.py
+++ b/solution.py
@@ -6,6 +6,22 @@
 SLOT = 128
 NBR = 32
 EPSILON = 1e-05
+
+
+def collect(x, axis, dim):
+    ways, here, step = (lax.axis_size(axis), lax.axis_index(axis), x.shape[dim])
+    shape = [n * ways if d == dim else n for d, n in enumerate(x.shape)]
+    full = lax.dynamic_update_slice_in_dim(jnp.zeros(shape, x.dtype), x, here * step, axis=dim)
+    going_up = going_down = x
+    for far in range(1, ways // 2 + 1):
+        going_up = lax.ppermute(going_up, axis, [(d, (d + 1) % ways) for d in range(ways)])
+        full = lax.dynamic_update_slice_in_dim(full, going_up, (here - far) % ways * step, axis=dim)
+        if 2 * far < ways:
+            going_down = lax.ppermute(going_down, axis, [(d, (d - 1) % ways) for d in range(ways)])
+            full = lax.dynamic_update_slice_in_dim(
+                full, going_down, (here + far) % ways * step, axis=dim
+            )
+    return full
 
 
 def build_tiles(neighbours):
@@ -44,7 +60,7 @@
 
 def forward_layer(values, weight, gamma, beta, tiles, self_weight, valid):
     mixed = spread(values, tiles, self_weight).astype(jnp.bfloat16)
-    gathered = lax.all_gather(mixed, "col", axis=1, tiled=True)
+    gathered = collect(mixed, "col", 1)
     linear = jnp.dot(gathered, weight, preferred_element_type=jnp.float32)
     total_valid, mean, variance = moments(linear, valid)
     inv_std = lax.rsqrt(variance + EPSILON)

time: 857 us -> 884 us (1.032)
  local copies, waits for them, and re-layouts: 18.1 us -> 28.6 us
  starting transfers between devices: 0.87 us -> 10.1 us
    ppermute x0 -> x6, waiting for transfers between devices: none -> 107 us  [the longest x4 107 us: collect(): lax.ppermute(going_up, axis, [(d, (d + 1) % ways) for d in range(ways)])]
    all_gather x2 -> x0, waiting for transfers between devices: 105 us -> none  [forward_layer(): gathered = lax.all_gather(mixed, 'col', axis=1, tiled=True)]
    ppermute x0 -> x6, starting transfers between devices: none -> 9.75 us  [the longest x4 6.06 us: collect(): lax.ppermute(going_up, axis, [(d, (d + 1) % ways) for d in range(ways)])]
  transfers between devices with their start and end apart: 5 -> 9, of which waited for: 5 -> 7; matrix products, arithmetic and copies ran while one was open for 3% -> 4% of each run, Pallas kernels for 0% -> 0%
where the time goes in v1:
time: 884 us; the launch traced here: 876 us
  waiting for transfers between devices  576 us (65%)
  blocking collectives  118 us (13%)
  matrix products  70.7 us (8%)
  other arithmetic  57.2 us (6%)
  local copies, waits for them, and re-layouts  28.6 us (3%)
  between operations  14.4 us (2%)
  starting transfers between devices  10.1 us (1%)
    psum x1, waiting for transfers between devices, backward_layer(): grad_weight = lax.psum(weight_terms, 'row')  267 us
    reduce_scatter x2, waiting for transfers between devices, backward_layer(): lax.psum_scatter(partial_terms, 'col', scatter_dimension=1, tiled=True)  202 us
    ppermute x4, waiting for transfers between devices, collect(): lax.ppermute(going_up, axis, [(d, (d + 1) % ways) for d in range(ways)])  107 us
    psum x2, blocking collectives, moments(): lax.psum((jnp.sum(valid), jnp.sum(valid * linear, axis=0)), 'row')  43.1 us
    psum x2, blocking collectives, backward_layer(): lax.psum((jnp.sum(grad_before, axis=0), jnp.sum(grad_before * normed, axi...  40.6 us
    psum x2, blocking collectives, moments(): lax.psum(jnp.sum(valid * centred * centred, axis=0), 'row') / total_valid  34.7 us
    dot_general x2, matrix products, backward_layer(): lax.dot_general(gathered, grad_low, (((0,), (0,)), ((), ())), preferred_e...  20.4 us
  transfers between devices with their start and end apart: 9, of which 7 were waited for; matrix products, arithmetic and copies ran while one was open for 4% of the time, Pallas kernels for 0%

profile of v1, /device:TPU:0, one launch (start us, length us, event | category | flops | bytes accessed | tf_op | source)
XLA Modules:
  0.0 875.8 jit_solution(12742616067314262111)
XLA Ops:
  7.3 2.3 copy.23
  9.6 27.6 %while.10 = (s32[]{:T(128)}, f32[14,128,128]{2,1,0:T(8,128)S(1)}, s32[14,128,32]{2,1,0:T(8,128)}, s32[]{:T(128)}) while((s32[]{:T(128)}, f32[14,128,128]{2,1,0:T(8,128)S(1)}, s32[14,128,32]{2,1,0:T(8,128)}, s32[]{:T(128)}) %tuple.43), condition=%wide.region_3.4_spmd, body=%wide.region_0.3_spmd.sunk | while | flops 1634306 | bytes 247877 | solution.py:37
  9.6 0.9 convert_reduce_fusion.5
  11.5 0.9 convert_reduce_fusion.5
  13.5 0.9 convert_reduce_fusion.5
  15.5 0.9 convert_reduce_fusion.5
  17.4 0.9 convert_reduce_fusion.5
  18.4 0.9 convert_reduce_fusion.6
  19.4 0.9 convert_reduce_fusion.5
  20.4 0.9 convert_reduce_fusion.6
  21.4 0.9 convert_reduce_fusion.5
  23.4 0.9 convert_reduce_fusion.5
  25.3 0.9 convert_reduce_fusion.5
  27.3 0.9 convert_reduce_fusion.5
  29.3 0.9 convert_reduce_fusion.5
  31.3 0.9 convert_reduce_fusion.5
  33.2 0.9 convert_reduce_fusion.5
  35.2 0.9 convert_reduce_fusion.5
  37.2 4.7 copy.24
  41.8 1.8 gather_fusion
  43.7 5.1 add_convert_fusion.1
  49.2 2.0 collective-permute-start.1
  51.2 38.2 %collective-permute-done = bf16[1792,512]{1,0:T(8,128)(2,1)} collective-permute-done((bf16[1792,512]{1,0:T(8,128)(2,1)}, bf16[1792,512]{1,0:T(8,128)(2,1)}, u32[]{:S(2)}, u32[]{:S(2)}) %collective-permute-start) | collective-permute-done | bytes 1835040 | tf_op jit(solution)/shard_map/ppermute | solution.py:17
  89.4 2.6 collective-permute-start.2
  92.6 0.9 broadcast.58.clone
  93.5 1.8 constant_dynamic-update-slice_fusion.7
  95.3 1.8 constant_dynamic-update-slice_fusion.6
  97.2 1.9 constant_dynamic-update-slice_fusion.5
  99.1 13.2 %collective-permute-done.2 = bf16[1792,512]{1,0:T(8,128)(2,1)} collective-permute-done((bf16[1792,512]{1,0:T(8,128)(2,1)}, bf16[1792,512]{1,0:T(8,128)(2,1)}, u32[]{:S(2)}, u32[]{:S(2)}) %collective-permute-start.2) | collective-permute-done | bytes 1835040 | tf_op jit(solution)/shard_map/ppermute | solution.py:17
  112.4 1.8 constant_dynamic-update-slice_fusion.4
  114.2 5.8 multiply_reduce_fusion.3
  120.0 23.9 %all-reduce.2 = (f32[512]{0:T(512)S(1)}, f32[]{:T(128)}) all-reduce(f32[512]{0:T(512)S(1)} %get-tuple-element.49, f32[]{:T(128)} %convert_reduce_fusion.2), channel_id=1, replica_groups=mesh['row'=8,'col'=4] {'row'}, use_global_device_ids=true, to_apply=%region_5.6 | all-reduce | flops 513 | bytes 4104 | tf_op jit(solution)/shard_map/psum | solution.py:54
  144.4 2.6 fusion.2
  147.0 17.6 %psum.82 = f32[512]{0:T(512)S(1)} all-reduce(f32[512]{0:T(512)S(1)} %fusion.2), channel_id=1, replica_groups=mesh['row'=8,'col'=4] {'row'}, use_global_device_ids=true, to_apply=%region_9.10 | all-reduce | flops 512 | bytes 4096 | tf_op jit(solution)/shard_map/psum | solution.py:57
  165.2 3.0 multiply_multiply_fusion.4
  168.2 3.8 add_convert_fusion
  172.1 1.7 collective-permute-start.4
  173.8 37.6 %collective-permute-done.3 = bf16[1792,512]{1,0:T(8,128)(2,1)S(1)} collective-permute-done((bf16[1792,512]{1,0:T(8,128)(2,1)S(1)}, bf16[1792,512]{1,0:T(8,128)(2,1)S(1)}, u32[]{:S(2)}, u32[]{:S(2)}) %collective-permute-start.3) | collective-permute-done | bytes 1835040 | tf_op jit(solution)/shard_map/ppermute | solution.py:17
  211.4 3.0 collective-permute-start.5
  214.3 0.9 broadcast.58
  216.2 17.8 %collective-permute-done.5 = bf16[1792,512]{1,0:T(8,128)(2,1)S(1)} collective-permute-done((bf16[1792,512]{1,0:T(8,128)(2,1)S(1)}, bf16[1792,512]{1,0:T(8,128)(2,1)S(1)}, u32[]{:S(2)}, u32[]{:S(2)}) %collective-permute-start.5) | collective-permute-done | bytes 1835040 | tf_op jit(solution)/shard_map/ppermute | solution.py:17
  234.4 5.8 multiply_reduce_fusion.2
  240.2 19.3 %psum.83 = f32[512]{0:T(512)S(1)} all-reduce(f32[512]{0:T(512)S(1)} %get-tuple-element.51), channel_id=1, replica_groups=mesh['row'=8,'col'=4] {'row'}, use_global_device_ids=true, to_apply=%region_11.12 | all-reduce | flops 512 | bytes 4096 | tf_op jit(solution)/shard_map/psum | solution.py:54
  260.0 2.6 fusion.3
  262.6 17.1 %psum.84 = f32[512]{0:T(512)S(1)} all-reduce(f32[512]{0:T(512)S(1)} %fusion.3), channel_id=1, replica_groups=mesh['row'=8,'col'=4] {'row'}, use_global_device_ids=true, to_apply=%region_13.14 | all-reduce | flops 512 | bytes 4096 | tf_op jit(solution)/shard_map/psum | solution.py:57
  280.4 6.3 fusion.6
  286.6 19.3 %all-reduce.1 = (f32[512]{0:T(512)S(1)}, f32[512]{0:T(512)S(1)}) all-reduce(f32[512]{0:T(512)S(1)} %get-tuple-element.29, f32[512]{0:T(512)S(1)} %get-tuple-element.28), channel_id=1, replica_groups=mesh['row'=8,'col'=4] {'row'}, use_global_device_ids=true, to_apply=%region_17.18 | all-reduce | flops 1024 | bytes 8192 | tf_op jit(solution)/shard_map/psum | solution.py:78
  305.9 4.5 multiply_convert_fusion.1
  310.5 1.2 copy-done.6
  311.7 7.2 fusion.8
  319.0 114.1 %reduce-scatter.3.cloned.1.call-done = f32[1792,512]{1,0:T(8,128)} async-done(((f32[1792,2048]{1,0:T(8,128)}), f32[1792,512]{1,0:T(8,128)}) %reduce-scatter.3.cloned.1.call-update) | async-done | bytes 3670032 | tf_op jit(solution)/shard_map/reduce_scatter | solution.py:93
  433.1 6.8 multiply_add_fusion.1
  439.9 3.7 fusion.5
  443.7 21.3 %all-reduce = (f32[512]{0:T(512)S(1)}, f32[512]{0:T(512)S(1)}) all-reduce(f32[512]{0:T(512)S(1)} %get-tuple-element.27, f32[512]{0:T(512)S(1)} %get-tuple-element.26), channel_id=1, replica_groups=mesh['row'=8,'col'=4] {'row'}, use_global_device_ids=true, to_apply=%region_22.23 | all-reduce | flops 1024 | bytes 8192 | tf_op jit(solution)/shard_map/psum | solution.py:78
  465.0 4.7 multiply_convert_fusion
  469.7 7.3 fusion.9
  477.3 1.2 copy-done.7
  478.5 9.9 %fusion.11 = f32[2048,512]{1,0:T(8,128)} fusion(bf16[1792,2048]{1,0:T(8,128)(2,1)} %copy-done.3, bf16[1792,512]{1,0:T(8,128)(2,1)S(1)} %copy-done.7), kind=kOutput, calls=%fused_computation.52 | convolution fusion | flops 3758096384 | bytes 13369344 | tf_op jit(solution)/shard_map/dot_general | solution.py:86
  488.4 10.5 %fusion.10 = f32[2048,512]{1,0:T(8,128)} fusion(bf16[1792,2048]{1,0:T(8,128)(2,1)} %copy-done.4, bf16[1792,512]{1,0:T(8,128)(2,1)S(1)} %copy-done.9), kind=kOutput, calls=%fused_computation.51 | convolution fusion | flops 3758096384 | bytes 13369344 | tf_op jit(solution)/shard_map/dot_general | solution.py:86
  498.9 87.5 %reduce-scatter.5.cloned.1.call-done = f32[1792,512]{1,0:T(8,128)} async-done(((f32[1792,2048]{1,0:T(8,128)}), f32[1792,512]{1,0:T(8,128)}) %reduce-scatter.5.cloned.1.call-update) | async-done | bytes 3670032 | tf_op jit(solution)/shard_map/reduce_scatter | solution.py:93
  586.4 8.5 multiply_add_fusion
  594.9 267.3 %all-reduce.6.cloned.1.call-done = (f32[2048,512]{1,0:T(8,128)}, f32[2048,512]{1,0:T(8,128)}) async-done(((f32[2048,512]{1,0:T(8,128)}, f32[2048,512]{1,0:T(8,128)}), (f32[2048,512]{1,0:T(8,128)}, f32[2048,512]{1,0:T(8,128)})) %all-reduce.6.cloned.1.call-update) | async-done | bytes 8388624 | tf_op jit(solution)/shard_map/psum | solution.py:89
  862.2 4.8 copy.47
  867.0 2.0 copy.48
  (105 shorter events, 17.2 us)
Async XLA Ops:
  7.2 227.2 %copy-start = (bf16[2048,512]{1,0:T(8,128)(2,1)S(1)}, bf16[2048,512]{1,0:T(8,128)(2,1)}, u32[]{:S(2)}) copy-start(bf16[2048,512]{1,0:T(8,128)(2,1)} %param.18) | copy-start | bytes 6291460
  7.2 425.9 %reduce-scatter.3.cloned.1.call-start = ((), (), s32[]{:S(2)}) async-start(), calls=%async_computation.2 | async-start | bytes 18350080 | tf_op jit(solution)/shard_map/reduce_scatter | solution.py:93
  41.8 50.2 %copy-start.10 = (s32[1792]{0:T(1024)S(1)}, s32[1792]{0:T(1024)}, u32[]{:S(2)}) copy-start(s32[1792]{0:T(1024)} %param.14) | copy-start | bytes 21508
  48.8 40.6 %collective-permute-start = (bf16[1792,512]{1,0:T(8,128)(2,1)}, bf16[1792,512]{1,0:T(8,128)(2,1)}, u32[]{:S(2)}, u32[]{:S(2)}) collective-permute-start(bf16[1792,512]{1,0:T(8,128)(2,1)} %bitcast.6), channel_id=1, source_target_pairs={{0,1},{1,2},{2,3},{3,0},{4,5},{5,6},{6,7},{7,4},{8,9},{9,10},{10,1... | collective-permute-start | bytes 5505032 | tf_op jit(solution)/shard_map/ppermute | solution.py:17
  49.2 47.9 %collective-permute-start.1 = (bf16[1792,512]{1,0:T(8,128)(2,1)}, bf16[1792,512]{1,0:T(8,128)(2,1)}, u32[]{:S(2)}, u32[]{:S(2)}) collective-permute-start(bf16[1792,512]{1,0:T(8,128)(2,1)} %bitcast.6), channel_id=1, source_target_pairs={{0,3},{1,0},{2,1},{3,2},{4,7},{5,4},{6,5},{7,6},{8,11},{9,8},{10,9... | collective-permute-start | bytes 5505032 | tf_op jit(solution)/shard_map/ppermute | solution.py:20
  89.4 23.0 %collective-permute-start.2 = (bf16[1792,512]{1,0:T(8,128)(2,1)}, bf16[1792,512]{1,0:T(8,128)(2,1)}, u32[]{:S(2)}, u32[]{:S(2)}) collective-permute-start(bf16[1792,512]{1,0:T(8,128)(2,1)} %collective-permute-done), channel_id=1, source_target_pairs={{0,1},{1,2},{2,3},{3,0},{4,5},{5,6},{6,7},{7,4},{8,9},{9,10},{10,1... | collective-permute-start | bytes 5505032 | tf_op jit(solution)/shard_map/ppermute | solution.py:17
  97.1 17.0 %copy-start.19 = (bf16[2048,512]{1,0:T(8,128)(2,1)S(1)}, bf16[2048,512]{1,0:T(8,128)(2,1)}, u32[]{:S(2)}) copy-start(bf16[2048,512]{1,0:T(8,128)(2,1)} %param.15) | copy-start | bytes 6291460
  114.2 5.8 copy-start.4
  120.0 45.2 %copy-start.11 = (f32[512]{0:T(512)S(1)}, f32[512]{0:T(512)}, u32[]{:S(2)}) copy-start(f32[512]{0:T(512)} %param.16) | copy-start | bytes 6148
  120.0 45.2 %copy-start.13 = (f32[512]{0:T(512)S(1)}, f32[512]{0:T(512)}, u32[]{:S(2)}) copy-start(f32[512]{0:T(512)} %param.17) | copy-start | bytes 6148
  172.0 39.4 %collective-permute-start.3 = (bf16[1792,512]{1,0:T(8,128)(2,1)S(1)}, bf16[1792,512]{1,0:T(8,128)(2,1)S(1)}, u32[]{:S(2)}, u32[]{:S(2)}) collective-permute-start(bf16[1792,512]{1,0:T(8,128)(2,1)S(1)} %bitcast.48), channel_id=1, source_target_pairs={{0,1},{1,2},{2,3},{3,0},{4,5},{5,6},{6,7},{7,4},{8,9},{9,10},{10,1... | collective-permute-start | bytes 5505032 | tf_op jit(solution)/shard_map/ppermute | solution.py:17
  172.1 43.8 %collective-permute-start.4 = (bf16[1792,512]{1,0:T(8,128)(2,1)S(1)}, bf16[1792,512]{1,0:T(8,128)(2,1)S(1)}, u32[]{:S(2)}, u32[]{:S(2)}) collective-permute-start(bf16[1792,512]{1,0:T(8,128)(2,1)S(1)} %bitcast.49), channel_id=1, source_target_pairs={{0,3},{1,0},{2,1},{3,2},{4,7},{5,4},{6,5},{7,6},{8,11},{9,8},{10,9... | collective-permute-start | bytes 5505032 | tf_op jit(solution)/shard_map/ppermute | solution.py:20
  211.4 22.7 %collective-permute-start.5 = (bf16[1792,512]{1,0:T(8,128)(2,1)S(1)}, bf16[1792,512]{1,0:T(8,128)(2,1)S(1)}, u32[]{:S(2)}, u32[]{:S(2)}) collective-permute-start(bf16[1792,512]{1,0:T(8,128)(2,1)S(1)} %collective-permute-done.3), channel_id=1, source_target_pairs={{0,1},{1,2},{2,3},{3,0},{4,5},{5,6},{6,7},{7,4},{8,9},{9,10},{10,1... | collective-permute-start | bytes 5505032 | tf_op jit(solution)/shard_map/ppermute | solution.py:17
  234.4 5.8 copy-start.3
  240.2 40.1 %copy-start.12 = (f32[512]{0:T(512)S(1)}, f32[512]{0:T(512)}, u32[]{:S(2)}) copy-start(f32[512]{0:T(512)} %param.19) | copy-start | bytes 6148
  240.2 40.1 %copy-start.14 = (f32[512]{0:T(512)S(1)}, f32[512]{0:T(512)}, u32[]{:S(2)}) copy-start(f32[512]{0:T(512)} %param.20) | copy-start | bytes 6148
  305.9 4.5 copy-start.15
  305.9 4.6 copy-start.17
  310.5 1.2 copy-start.6
  319.0 267.5 %reduce-scatter.5.cloned.1.call-start = ((), (), s32[]{:S(2)}) async-start(), calls=%async_computation.3 | async-start | bytes 18350080 | tf_op jit(solution)/shard_map/reduce_scatter | solution.py:93
  433.1 6.8 copy-start.2
  465.0 4.7 copy-start.16
  465.0 4.7 copy-start.18
  465.0 4.7 copy-start.20
  469.7 7.3 copy-start.8
  477.0 1.5 copy-start.7
  477.0 385.2 %all-reduce.6.cloned.1.call-start = ((), (), s32[]{:S(2)}) async-start(), calls=%async_computation.4 | async-start | bytes 16777216 | tf_op jit(solution)/shard_map/psum | solution.py:89
  478.5 9.9 %copy-start.9 = (bf16[1792,512]{1,0:T(8,128)(2,1)S(1)}, bf16[1792,512]{1,0:T(8,128)(2,1)}, u32[]{:S(2)}) copy-start(bf16[1792,512]{1,0:T(8,128)(2,1)} %copy-done.8) | copy-start | bytes 5505028
  862.2 4.8 copy-start.5
  862.2 6.8 copy-start.1
Sparse Core Ops, SparseCore 0:
  319.1 113.9 reduce-scatter.2
  477.1 109.2 reduce-scatter.4
  591.1 271.0 all-reduce.5
